TPU v7x, 128 devices: a whole 4x4x4 slice. The times are simulated.
128 devices in a mesh: dp: 16 (over x, y), expert: 8 (over z, core).
Axes of the slice: x: 4, y: 4, z: 4, core: 2. Of those that a mesh axis runs over, the one named last changes fastest.
Arguments:
- tokens: bfloat16 [2048, 4096], P('dp', 'expert'), may hold values from -6 to 6
- output_gradient: bfloat16 [2048, 4096], P('dp', 'expert'), may hold values from -6 to 6
- routing: int32 [2048, 2], P('dp'), may hold values from 0 to 7, all different within a row; in each aligned block of 128 rows (0 to 127, 128 to 255, ...) at most 96 rows name the same one
- router_gate_values: float32 [2048, 2], P('dp'), may hold values from 0.1 to 0.9
- gate_weight: bfloat16 [8, 7168, 4096], P('expert', 'dp'), may hold values from -0.09375 to 0.09375
- up_weight: bfloat16 [8, 7168, 4096], P('expert', 'dp'), may hold values from -0.09375 to 0.09375
- down_weight: bfloat16 [8, 7168, 4096], P('expert', 'dp'), may hold values from -0.0625 to 0.0625
- adapter_lower_gate: bfloat16 [8, 16, 4096], P('expert'), may hold values from -0.09375 to 0.09375
- adapter_upper_gate: bfloat16 [8, 7168, 16], P('expert', 'dp'), may hold values from -0.375 to 0.375
- adapter_lower_up: bfloat16 [8, 16, 4096], P('expert'), may hold values from -0.09375 to 0.09375
- adapter_upper_up: bfloat16 [8, 7168, 16], P('expert', 'dp'), may hold values from -0.375 to 0.375
- adapter_lower_down: bfloat16 [8, 16, 7168], P('expert', None, 'dp'), may hold values from -0.0625 to 0.0625
- adapter_upper_down: bfloat16 [8, 4096, 16], P('expert'), may hold values from -0.375 to 0.375
Outputs:
- grad_x: bfloat16 [2048, 4096], P('dp', 'expert')
- grad_lora_a_gate: float32 [8, 16, 4096], P('expert')
- grad_lora_b_gate: float32 [8, 7168, 16], P('expert', 'dp')
- grad_lora_a_up: float32 [8, 16, 4096], P('expert')
- grad_lora_b_up: float32 [8, 7168, 16], P('expert', 'dp')
- grad_lora_a_down: float32 [8, 16, 7168], P('expert', None, 'dp')
- grad_lora_b_down: float32 [8, 4096, 16], P('expert')
Inputs may be any that keep to these rules, and one draw needn't show every extreme that they name: `routing`: each row names two different experts. In the rows of one dp shard (aligned blocks of 128 rows) no expert is named by more than 96 rows, and in some blocks one expert is named by exactly 96 rows.
All inputs are finite; a program needn't handle non-finite values.
Results may differ from a plain program's by a relative error of at most 0.015.
Values may be sent and summed in bfloat16 or wider, within the bound.
A program may use at most 256 MiB of HBM per device.

v0:
```python
import jax
import jax.numpy as jnp
from jax import lax
from jax.sharding import PartitionSpec as P

ADAPTER_SCALE = 2.0
NUM_CHUNKS = 2


def contract_pair(left, right, left_axis, right_axis):
    return lax.dot_general(
        left, right, (((left_axis,), (right_axis,)), ((), ())), preferred_element_type=jnp.float32
    )


def slot_numbers(route_rows, experts):
    picked = (route_rows[:, :, None] == jnp.arange(experts, dtype=jnp.int32)[None, None, :]).astype(
        jnp.int32
    )
    per_token = jnp.sum(picked, axis=1)
    earlier = jnp.cumsum(per_token, axis=0) - per_token
    return jnp.sum(earlier[:, None, :] * picked, axis=2)


def slot_sources(route_rows, positions, experts, capacity):
    tokens_here, choose = route_rows.shape
    target = (route_rows * capacity + positions).reshape(-1)
    owners = jnp.repeat(jnp.arange(tokens_here, dtype=jnp.int32), choose)
    member_ids = jnp.tile(jnp.arange(choose, dtype=jnp.int32), tokens_here)
    source = jnp.full((experts * capacity,), tokens_here, jnp.int32).at[target].set(owners)
    member = jnp.zeros((experts * capacity,), jnp.int32).at[target].set(member_ids)
    return (source, member)


def rows_backward_pass(input_rows, output_gradient_rows, params):
    (
        gate_weight,
        up_weight,
        down_weight,
        a_gate,
        gate_adapter_upper,
        a_up,
        up_adapter_upper,
        down_adapter_lower,
        b_down,
    ) = params
    gate_projected_lower = contract_pair(a_gate, input_rows, 1, 1).astype(jnp.bfloat16)
    up_projected_lower = contract_pair(a_up, input_rows, 1, 1).astype(jnp.bfloat16)
    gate_preactivation = contract_pair(
        gate_weight, input_rows, 1, 1
    ) + ADAPTER_SCALE * contract_pair(gate_adapter_upper, gate_projected_lower, 1, 0)
    up_preactivation = contract_pair(up_weight, input_rows, 1, 1) + ADAPTER_SCALE * contract_pair(
        up_adapter_upper, up_projected_lower, 1, 0
    )
    sigmoid_gate = jax.nn.sigmoid(gate_preactivation)
    silu_gate = gate_preactivation * sigmoid_gate
    hidden_units = (silu_gate * up_preactivation).astype(jnp.bfloat16)
    down_projected_lower = contract_pair(b_down, output_gradient_rows, 0, 1).astype(jnp.bfloat16)
    hidden_gradient = contract_pair(
        down_weight, output_gradient_rows, 1, 1
    ) + ADAPTER_SCALE * contract_pair(down_adapter_lower, down_projected_lower, 0, 0)
    gate_gradient = (
        hidden_gradient
        * up_preactivation
        * sigmoid_gate
        * (1.0 + gate_preactivation * (1.0 - sigmoid_gate))
    ).astype(jnp.bfloat16)
    up_gradient = (hidden_gradient * silu_gate).astype(jnp.bfloat16)
    gate_partial = contract_pair(gate_adapter_upper, gate_gradient, 0, 0).astype(jnp.bfloat16)
    up_partial = contract_pair(up_adapter_upper, up_gradient, 0, 0).astype(jnp.bfloat16)
    down_partial = contract_pair(down_adapter_lower, hidden_units, 1, 0).astype(jnp.bfloat16)
    paired_partials = jnp.concatenate([gate_partial, up_partial], 0)
    paired_factors = jnp.concatenate([a_gate, a_up], 0)
    gradient_rows_out = (
        contract_pair(gate_gradient, gate_weight, 0, 0)
        + contract_pair(up_gradient, up_weight, 0, 0)
        + ADAPTER_SCALE * contract_pair(paired_partials, paired_factors, 0, 0)
    )
    shared_slice = (
        ADAPTER_SCALE * contract_pair(gate_partial, input_rows, 1, 0),
        ADAPTER_SCALE * contract_pair(up_partial, input_rows, 1, 0),
        ADAPTER_SCALE * contract_pair(output_gradient_rows, down_partial, 0, 1),
    )
    owned_slice = (
        ADAPTER_SCALE * contract_pair(gate_gradient, gate_projected_lower, 1, 1),
        ADAPTER_SCALE * contract_pair(up_gradient, up_projected_lower, 1, 1),
        ADAPTER_SCALE * contract_pair(down_projected_lower, hidden_units, 1, 1),
    )
    return (gradient_rows_out, shared_slice, owned_slice)


def local(
    tokens,
    output_gradient,
    routing,
    router_gate_values,
    gate_weight,
    up_weight,
    down_weight,
    adapter_lower_gate,
    adapter_upper_gate,
    adapter_lower_up,
    adapter_upper_up,
    adapter_lower_down,
    adapter_upper_down,
):
    experts = lax.axis_size("expert")
    shards = lax.axis_size("dp")
    tok_local, feat_local = tokens.shape
    choose = routing.shape[1]
    complete_width = feat_local * experts
    capacity = min(tok_local, 6 * tok_local // experts)
    adapter_rank = adapter_lower_gate.shape[1]
    chunks = NUM_CHUNKS
    piece = capacity // chunks
    params = (
        gate_weight[0],
        up_weight[0],
        down_weight[0],
        adapter_lower_gate[0],
        adapter_upper_gate[0],
        adapter_lower_up[0],
        adapter_upper_up[0],
        adapter_lower_down[0],
        adapter_upper_down[0],
    )
    positions = slot_numbers(routing, experts)
    zero_row = jnp.zeros((1, feat_local), jnp.bfloat16)
    source, member = slot_sources(routing, positions, experts, capacity)
    clamped = jnp.minimum(source, tok_local - 1)
    slot_gate = jnp.where(
        source < tok_local, router_gate_values.reshape(-1)[clamped * choose + member], 0.0
    )
    send_x = jnp.concatenate([tokens, zero_row], 0)[source].reshape(experts, capacity, feat_local)
    send_dy = (
        (
            slot_gate[:, None]
            * jnp.concatenate([output_gradient, zero_row], 0)[source].astype(jnp.float32)
        )
        .astype(jnp.bfloat16)
        .reshape(experts, capacity, feat_local)
    )
    send_both = jnp.concatenate([send_x, send_dy], axis=2)
    recv_both = lax.all_to_all(send_both, "expert", split_axis=0, concat_axis=2, tiled=True)[0]
    recv_both = recv_both.reshape(capacity, experts, 2, feat_local).transpose(0, 2, 1, 3)
    recv_both = recv_both.reshape(capacity, 2 * complete_width)
    rows_pieces = []
    shared_total = None
    owned_total = None
    for c in range(chunks):
        part = recv_both[c * piece : (c + 1) * piece]
        gathered = lax.all_gather(part, "dp", axis=0, tiled=True)
        x_rows = gathered[:, :complete_width]
        dy_rows = gathered[:, complete_width:]
        rows_out, shared_slice, owned_slice = rows_backward_pass(x_rows, dy_rows, params)
        if c == 0:
            shared_total, owned_total = (shared_slice, owned_slice)
        else:
            shared_total = jax.tree.map(jnp.add, shared_total, shared_slice)
            owned_total = jax.tree.map(jnp.add, owned_total, owned_slice)
        rows_bf = rows_out.astype(jnp.bfloat16).reshape(shards, piece, complete_width)
        summed = lax.psum_scatter(rows_bf, "dp", scatter_dimension=0, tiled=True)[0]
        rows_pieces.append(summed)
    lora = jnp.concatenate([shared_total[0], shared_total[1], shared_total[2].T], 0).astype(
        jnp.bfloat16
    )
    lora_shape = lora.shape
    lora_part = lax.psum_scatter(
        lora.reshape(shards * 8, -1), "dp", scatter_dimension=0, tiled=True
    )
    summed = jnp.concatenate(rows_pieces, 0)
    lora_part = lax.optimization_barrier(lora_part)
    lora_sum = lax.all_gather(lora_part, "dp", axis=0, tiled=True).astype(jnp.float32)
    lora_sum = lora_sum.reshape(lora_shape)
    grad_a_gate = lora_sum[:adapter_rank]
    grad_a_up = lora_sum[adapter_rank : 2 * adapter_rank]
    grad_b_down = lora_sum[2 * adapter_rank :].T
    returned_rows = lax.all_to_all(
        summed.reshape(capacity, experts, feat_local),
        "expert",
        split_axis=1,
        concat_axis=1,
        tiled=True,
    ).astype(jnp.float32)
    lookup = positions * experts + routing
    grad_x = jnp.sum(returned_rows.reshape(capacity * experts, feat_local)[lookup], axis=1).astype(
        jnp.bfloat16
    )
    return (
        grad_x,
        grad_a_gate[None],
        owned_total[0][None],
        grad_a_up[None],
        owned_total[1][None],
        owned_total[2][None],
        grad_b_down[None],
    )


def solution(mesh):
    return jax.shard_map(
        local,
        mesh=mesh,
        in_specs=(
            P("dp", "expert"),
            P("dp", "expert"),
            P("dp", None),
            P("dp", None),
            P("expert", "dp", None),
            P("expert", "dp", None),
            P("expert", "dp", None),
            P("expert", None, None),
            P("expert", "dp", None),
            P("expert", None, None),
            P("expert", "dp", None),
            P("expert", None, "dp"),
            P("expert", None, None),
        ),
        out_specs=(
            P("dp", "expert"),
            P("expert", None, None),
            P("expert", "dp", None),
            P("expert", None, None),
            P("expert", "dp", None),
            P("expert", None, "dp"),
            P("expert", None, None),
        ),
        check_vma=False,
    )
```

profile of v0, /device:TPU:1, one launch (start us, length us, event | category | flops | bytes accessed | tf_op | source)
XLA Modules:
  0.0 568.4 jit_solution(9020184322485059997)
XLA Ops:
  9.1 1.3 compare_select_fusion.3
  11.8 1.4 scatter_custom_fusion.1
  13.3 1.4 scatter_custom_fusion
  14.7 5.0 gather_fusion.1
  19.8 2.7 gather_fusion.2
  22.5 2.7 gather_fusion
  25.7 27.4 %all_to_all.20 = bf16[8,96,1024]{2,1,0:T(8,128)(2,1)S(1)} all-to-all(bf16[8,96,1024]{2,1,0:T(8,128)(2,1)S(1)} %pad_maximum_fusion), channel_id=1, replica_groups=mesh['dp'=16,'expert'=8] {'expert'}, dimensions={0} | all-to-all | bytes 3145728 | tf_op jit(solution)/shard_map/all_to_all | solution.py:144
  54.2 1.7 copy.71
  56.0 1.3 fusion.132
  57.5 1.3 copy.65
  59.0 1.3 copy.67
  60.7 88.0 %all-gather.3.cloned.1.call-done = bf16[768,8192]{1,0:T(8,128)(2,1)} async-done(((bf16[48,8192]{1,0:T(8,128)(2,1)}), bf16[768,8192]{1,0:T(8,128)(2,1)}) %all-gather.3.cloned.1.call-update) | async-done | bytes 12582928 | tf_op jit(solution)/shard_map/all_gather | solution.py:152
  148.7 4.7 fusion.79
  153.4 6.0 %fusion.31 = f32[768,448]{0,1:T(8,128)S(1)} fusion(bf16[1,448,4096]{2,1,0:T(8,128)(2,1)S(1)} %copy-done.2, bf16[768,8192]{1,0:T(8,128)(2,1)} %all-gather.3.cloned.1.call-done), kind=kOutput, calls=%fused_computation.35 | convolution fusion | flops 2818572288 | bytes 11337728 | tf_op jit(solution)/shard_map/dot_general | solution.py:11
  159.9 1.7 fusion.88
  162.3 3.1 fusion.10
  165.8 1.7 fusion.76
  167.9 14.7 %fusion.39 = f32[768,448]{0,1:T(8,128)S(1)} fusion(bf16[1,448,4096]{2,1,0:T(8,128)(2,1)S(1)} %copy-done.4, bf16[768,8192]{1,0:T(8,128)(2,1)S(1)} %bitcast.166), kind=kOutput, calls=%fused_computation.43 | convolution fusion | flops 2818572288 | bytes 11337728 | tf_op jit(solution)/shard_map/dot_general | solution.py:11
  182.6 1.8 multiply_convert_fusion.1
  184.8 6.6 %fusion.29 = f32[768,4096]{1,0:T(8,128)} fusion(bf16[448,768]{1,0:T(8,128)(2,1)S(1)} %get-tuple-element.8, bf16[1,448,4096]{2,1,0:T(8,128)(2,1)S(1)} %copy-done.2), kind=kOutput, calls=%fused_computation.33 | convolution fusion | flops 2818572288 | bytes 16941056 | tf_op jit(solution)/shard_map/dot_general | solution.py:11
  191.4 6.5 %fusion.37 = f32[768,4096]{1,0:T(8,128)} fusion(bf16[448,768]{1,0:T(8,128)(2,1)S(1)} %get-tuple-element.9, bf16[1,448,4096]{2,1,0:T(8,128)(2,1)S(1)} %copy-done.4), kind=kOutput, calls=%fused_computation.41 | convolution fusion | flops 2818572288 | bytes 16941056 | tf_op jit(solution)/shard_map/dot_general | solution.py:11
  197.9 42.7 %all-gather.5.cloned.1.call-done = bf16[768,8192]{1,0:T(8,128)(2,1)} async-done(((bf16[48,8192]{1,0:T(8,128)(2,1)}), bf16[768,8192]{1,0:T(8,128)(2,1)}) %all-gather.5.cloned.1.call-update) | async-done | bytes 12582928 | tf_op jit(solution)/shard_map/all_gather | solution.py:152
  240.5 4.7 fusion.91
  245.2 6.0 %fusion.4 = f32[768,448]{0,1:T(8,128)S(1)} fusion(bf16[768,8192]{1,0:T(8,128)(2,1)} %all-gather.5.cloned.1.call-done, bf16[1,448,4096]{2,1,0:T(8,128)(2,1)S(1)} %copy-done.35), kind=kOutput, calls=%fused_computation.12 | convolution fusion | flops 2818572288 | bytes 11337728 | tf_op jit(solution)/shard_map/dot_general | solution.py:11
  251.7 1.7 fusion.85
  253.7 3.1 fusion.27
  257.2 1.7 fusion.82
  259.2 3.3 fusion.35
  262.5 1.8 multiply_convert_fusion
  265.0 1.6 fusion.53
  267.6 4.1 fusion
  271.7 4.4 fusion.23
  276.0 4.4 fusion.24
  280.4 4.1 fusion.20
  285.5 1.2 convert_element_type.133
  286.9 12.2 %add_convert_fusion.1 = bf16[768,4096]{1,0:T(8,128)(2,1)} fusion(f32[768,4096]{1,0:T(8,128)} %fusion.29, f32[768,4096]{1,0:T(8,128)} %fusion.37, bf16[16,4096]{1,0:T(8,128)(2,1)S(1)} %bitcast.186, bf16[16,4096]{1,0:T(8,128)(2,1)S(1)} %bitcast.184, bf16[16,768]{1,0:T(8,128)(2,1)} %bitcast.191, bf16[16,768]{1,0:T(8,128)(2,1)} %bitcast.190), kind=kOutput, calls=%fused_computation.7 | convolution fusion | flops 214532096 | bytes 31768576 | tf_op jit(solution)/shard_map/dot_general | solution.py:11
  299.2 8.9 %fusion.25 = f32[768,4096]{1,0:T(8,128)} fusion(bf16[448,768]{1,0:T(8,128)(2,1)S(1)} %get-tuple-element.11, bf16[1,448,4096]{2,1,0:T(8,128)(2,1)} %param.17), kind=kOutput, calls=%fused_computation.29 | convolution fusion | flops 2818572288 | bytes 16941056 | tf_op jit(solution)/shard_map/dot_general | solution.py:11
  308.1 6.4 %fusion.33 = f32[768,4096]{1,0:T(8,128)} fusion(bf16[448,768]{1,0:T(8,128)(2,1)S(1)} %get-tuple-element.12, bf16[1,448,4096]{2,1,0:T(8,128)(2,1)S(1)} %copy-done.6), kind=kOutput, calls=%fused_computation.37 | convolution fusion | flops 2818572288 | bytes 16941056 | tf_op jit(solution)/shard_map/dot_general | solution.py:11
  314.5 12.1 %add_convert_fusion = bf16[768,4096]{1,0:T(8,128)(2,1)} fusion(f32[768,4096]{1,0:T(8,128)} %fusion.25, f32[768,4096]{1,0:T(8,128)} %fusion.33, bf16[16,4096]{1,0:T(8,128)(2,1)S(1)} %bitcast.187, bf16[16,4096]{1,0:T(8,128)(2,1)S(1)} %bitcast.185, bf16[16,768]{1,0:T(8,128)(2,1)S(1)} %bitcast.193, bf16[16,768]{1,0:T(8,128)(2,1)S(1)} %bitcast.192), kind=kOutput, calls=%fused_computation.6 | convolution fusion | flops 214532096 | bytes 31768576 | tf_op jit(solution)/shard_map/dot_general | solution.py:11
  328.8 1.4 fusion.135
  330.2 2.1 fusion.95
  334.8 34.6 %all-reduce.7.cloned.1.call-done = bf16[128,1536]{1,0:T(8,128)(2,1)} async-done(((bf16[128,1536]{1,0:T(8,128)(2,1)}), bf16[128,1536]{1,0:T(8,128)(2,1)}) %all-reduce.7.cloned.1.call-update) | async-done | bytes 393232
  370.1 18.3 %all_gather.11 = bf16[128,1536]{1,0:T(8,128)(2,1)S(1)} all-gather(bf16[8,1536]{1,0:T(8,128)(2,1)S(1)} %constant_dynamic-slice_fusion), channel_id=1, replica_groups=mesh['dp'=16,'expert'=8] {'dp'}, dimensions={0}, use_global_device_ids=true | all-gather | bytes 417792 | tf_op jit(solution)/shard_map/all_gather | solution.py:173
  388.9 65.0 %reduce-scatter.7.cloned.1.call-done = bf16[1,48,4096]{2,1,0:T(8,128)(2,1)} async-done(((bf16[16,48,4096]{2,1,0:T(8,128)(2,1)}), bf16[1,48,4096]{2,1,0:T(8,128)(2,1)}) %reduce-scatter.7.cloned.1.call-update) | async-done | bytes 393232
  455.1 82.5 %reduce-scatter.9.cloned.1.call-done = bf16[1,48,4096]{2,1,0:T(8,128)(2,1)} async-done(((bf16[16,48,4096]{2,1,0:T(8,128)(2,1)}), bf16[1,48,4096]{2,1,0:T(8,128)(2,1)}) %reduce-scatter.9.cloned.1.call-update) | async-done | bytes 393232
  539.9 6.2 %all-to-all-start.1 = ((bf16[96,8,512]{2,0,1:T(8,128)(2,1)}), bf16[96,8,512]{2,0,1:T(8,128)(2,1)S(1)}, u32[]{:S(2)}, u32[]{:S(2)}) async-start(bf16[96,8,512]{2,0,1:T(8,128)(2,1)} %pad_maximum_fusion.1), calls=%async_computation.1 | async-start | bytes 1572864 | tf_op jit(solution)/shard_map/all_to_all | solution.py:178
  547.0 11.4 %all-to-all-done.1 = bf16[96,8,512]{2,0,1:T(8,128)(2,1)S(1)} async-done(((bf16[96,8,512]{2,0,1:T(8,128)(2,1)}), bf16[96,8,512]{2,0,1:T(8,128)(2,1)S(1)}, u32[]{:S(2)}, u32[]{:S(2)}) %all-to-all-start.1) | async-done | bytes 786464 | tf_op jit(solution)/shard_map/all_to_all | solution.py:178
  560.1 1.3 reduce_sum.29
  (160 shorter events, 23.3 us)
Async XLA Ops:
  7.2 152.7 %copy-start = (bf16[1,4096,16]{1,2,0:T(8,128)(2,1)S(1)}, bf16[1,4096,16]{1,2,0:T(8,128)(2,1)}, u32[]{:S(2)}) copy-start(bf16[1,4096,16]{1,2,0:T(8,128)(2,1)} %param.25) | copy-start | bytes 393220
  7.2 12.6 %copy-start.18 = (bf16[128,512]{1,0:T(8,128)(2,1)S(1)}, bf16[128,512]{1,0:T(8,128)(2,1)}, u32[]{:S(2)}) copy-start(bf16[128,512]{1,0:T(8,128)(2,1)} %param.14) | copy-start | bytes 393220
  7.2 12.6 %copy-start.19 = (bf16[128,512]{1,0:T(8,128)(2,1)S(1)}, bf16[128,512]{1,0:T(8,128)(2,1)}, u32[]{:S(2)}) copy-start(bf16[128,512]{1,0:T(8,128)(2,1)} %param.13) | copy-start | bytes 393220
  7.2 141.5 %all-gather.3.cloned.1.call-start = ((), (), s32[]{:S(2)}) async-start(), calls=%async_computation.4 | async-start | bytes 13369344 | tf_op jit(solution)/shard_map/all_gather | solution.py:152
  57.3 91.4 %copy-start.7 = (bf16[1,16,4096]{2,1,0:T(8,128)(2,1)S(1)}, bf16[1,16,4096]{2,1,0:T(8,128)(2,1)}, u32[]{:S(2)}) copy-start(bf16[1,16,4096]{2,1,0:T(8,128)(2,1)} %param.20) | copy-start | bytes 393220
  58.8 181.7 %all-gather.5.cloned.1.call-start = ((), (), s32[]{:S(2)}) async-start(), calls=%async_computation.5 | async-start | bytes 13369344 | tf_op jit(solution)/shard_map/all_gather | solution.py:152
  60.4 309.0 %all-reduce.7.cloned.1.call-start = ((), (), s32[]{:S(2)}) async-start(), calls=%async_computation.6 | async-start | bytes 786432
  148.7 4.7 copy-start.2
  148.7 11.1 %slice-start = ((s8[12582912]{0:T(1024)(128)(4,1)}), s8[4194304]{0:T(1024)(128)(4,1)S(1)}, s32[]{:S(2)}) async-start(s8[12582912]{0:T(1024)(128)(4,1)} %bitcast.165), calls=%async_computation.9 | async-start | bytes 8388608
  153.4 6.0 %copy-start.20 = (bf16[768,16]{0,1:T(8,128)(2,1)}, bf16[768,16]{0,1:T(8,128)(2,1)S(1)}, u32[]{:S(2)}) copy-start(bf16[768,16]{0,1:T(8,128)(2,1)S(1)} %fusion.79) | copy-start | bytes 73732
  153.4 6.0 %copy-start.11 = (bf16[1,448,16]{1,2,0:T(8,128)(2,1)S(1)}, bf16[1,448,16]{1,2,0:T(8,128)(2,1)}, u32[]{:S(2)}) copy-start(bf16[1,448,16]{1,2,0:T(8,128)(2,1)} %param.21) | copy-start | bytes 43012
  153.4 6.4 %slice-start.1 = ((s8[12582912]{0:T(1024)(128)(4,1)}), s8[4194304]{0:T(1024)(128)(4,1)S(1)}, s32[]{:S(2)}) async-start(s8[12582912]{0:T(1024)(128)(4,1)} %bitcast.165), calls=%async_computation.10 | async-start | bytes 8388608
  153.4 6.4 %slice-start.2 = ((s8[12582912]{0:T(1024)(128)(4,1)}), s8[4194304]{0:T(1024)(128)(4,1)S(1)}, s32[]{:S(2)}) async-start(s8[12582912]{0:T(1024)(128)(4,1)} %bitcast.165), calls=%async_computation.11 | async-start | bytes 8388608
  159.9 2.4 copy-start.34
  162.3 3.1 copy-start.22
  162.3 3.1 copy-start.10
  162.3 3.5 copy-start.8
  165.8 2.1 copy-start.4
  167.9 14.7 %copy-start.29 = (bf16[768,16]{0,1:T(8,128)(2,1)}, bf16[768,16]{0,1:T(8,128)(2,1)S(1)}, u32[]{:S(2)}) copy-start(bf16[768,16]{0,1:T(8,128)(2,1)S(1)} %fusion.76) | copy-start | bytes 73732
  167.9 14.7 %copy-start.28 = (bf16[1,448,16]{1,2,0:T(8,128)(2,1)S(1)}, bf16[1,448,16]{1,2,0:T(8,128)(2,1)}, u32[]{:S(2)}) copy-start(bf16[1,448,16]{1,2,0:T(8,128)(2,1)} %param.23) | copy-start | bytes 43012
  184.6 80.2 %copy-start.12 = (bf16[768,16]{0,1:T(8,128)(2,1)}, bf16[768,16]{0,1:T(8,128)(2,1)S(1)}, u32[]{:S(2)}) copy-start(bf16[768,16]{0,1:T(8,128)(2,1)S(1)} %convolution_convert_fusion.5) | copy-start | bytes 73732
  184.8 81.9 %copy-start.13 = (bf16[768,16]{0,1:T(8,128)(2,1)}, bf16[768,16]{0,1:T(8,128)(2,1)S(1)}, u32[]{:S(2)}) copy-start(bf16[768,16]{0,1:T(8,128)(2,1)S(1)} %convolution_convert_fusion.4) | copy-start | bytes 73732
  240.5 4.7 copy-start.35
  240.5 11.1 %slice-start.6 = ((s8[12582912]{0:T(1024)(128)(4,1)}), s8[4194304]{0:T(1024)(128)(4,1)S(1)}, s32[]{:S(2)}) async-start(s8[12582912]{0:T(1024)(128)(4,1)} %bitcast.169), calls=%async_computation.15 | async-start | bytes 8388608
  245.2 6.0 %copy-start.26 = (bf16[768,16]{0,1:T(8,128)(2,1)}, bf16[768,16]{0,1:T(8,128)(2,1)S(1)}, u32[]{:S(2)}) copy-start(bf16[768,16]{0,1:T(8,128)(2,1)S(1)} %fusion.91) | copy-start | bytes 73732
  245.2 6.4 %slice-start.7 = ((s8[12582912]{0:T(1024)(128)(4,1)}), s8[4194304]{0:T(1024)(128)(4,1)S(1)}, s32[]{:S(2)}) async-start(s8[12582912]{0:T(1024)(128)(4,1)} %bitcast.169), calls=%async_computation.16 | async-start | bytes 8388608
  245.2 6.4 %slice-start.8 = ((s8[12582912]{0:T(1024)(128)(4,1)}), s8[4194304]{0:T(1024)(128)(4,1)S(1)}, s32[]{:S(2)}) async-start(s8[12582912]{0:T(1024)(128)(4,1)} %bitcast.169), calls=%async_computation.17 | async-start | bytes 8388608
  253.7 3.1 copy-start.24
  259.2 3.3 copy-start.31
  259.2 5.5 slice-start.3
  259.2 5.6 slice-start.4
  262.5 2.5 slice-start.5
  264.5 7.1 %copy-start.14 = (bf16[768,16]{0,1:T(8,128)(2,1)}, bf16[768,16]{0,1:T(8,128)(2,1)S(1)}, u32[]{:S(2)}) copy-start(bf16[768,16]{0,1:T(8,128)(2,1)S(1)} %convolution_convert_fusion.3) | copy-start | bytes 73732
  265.0 11.1 %copy-start.16 = (bf16[768,16]{0,1:T(8,128)(2,1)}, bf16[768,16]{0,1:T(8,128)(2,1)S(1)}, u32[]{:S(2)}) copy-start(bf16[768,16]{0,1:T(8,128)(2,1)S(1)} %convolution_convert_fusion.2) | copy-start | bytes 73732
  280.4 6.4 %copy-start.9 = (bf16[1,16,4096]{2,1,0:T(8,128)(2,1)S(1)}, bf16[1,16,4096]{2,1,0:T(8,128)(2,1)}, u32[]{:S(2)}) copy-start(bf16[1,16,4096]{2,1,0:T(8,128)(2,1)} %param.22) | copy-start | bytes 393220
  286.8 167.1 %reduce-scatter.7.cloned.1.call-start = ((), (), s32[]{:S(2)}) async-start(), calls=%async_computation.7 | async-start | bytes 6684672
  299.1 238.5 %reduce-scatter.9.cloned.1.call-start = ((), (), s32[]{:S(2)}) async-start(), calls=%async_computation.8 | async-start | bytes 6684672
  299.2 8.9 %copy-start.6 = (bf16[1,448,4096]{2,1,0:T(8,128)(2,1)S(1)}, bf16[1,448,4096]{2,1,0:T(8,128)(2,1)}, u32[]{:S(2)}) copy-start(bf16[1,448,4096]{2,1,0:T(8,128)(2,1)} %param.18) | copy-start | bytes 11010052
  308.1 6.4 %copy-start.15 = (bf16[768,16]{0,1:T(8,128)(2,1)S(1)}, bf16[768,16]{0,1:T(8,128)(2,1)}, u32[]{:S(2)}) copy-start(bf16[768,16]{0,1:T(8,128)(2,1)} %copy-done.14) | copy-start | bytes 73732
  308.1 6.4 %copy-start.17 = (bf16[768,16]{0,1:T(8,128)(2,1)S(1)}, bf16[768,16]{0,1:T(8,128)(2,1)}, u32[]{:S(2)}) copy-start(bf16[768,16]{0,1:T(8,128)(2,1)} %copy-done.16) | copy-start | bytes 73732
  326.6 2.2 copy-start.23
  326.6 3.6 copy-start.27
  326.7 5.6 copy-start.30
  326.7 5.9 %copy-start.32 = (bf16[768,16]{0,1:T(8,128)(2,1)S(1)}, bf16[768,16]{0,1:T(8,128)(2,1)}, u32[]{:S(2)}) copy-start(bf16[768,16]{0,1:T(8,128)(2,1)} %copy-done.31) | copy-start | bytes 73732
  326.7 6.9 %copy-start.21 = (bf16[768,16]{0,1:T(8,128)(2,1)S(1)}, bf16[768,16]{0,1:T(8,128)(2,1)}, u32[]{:S(2)}) copy-start(bf16[768,16]{0,1:T(8,128)(2,1)} %copy-done.20) | copy-start | bytes 73732
  326.7 7.2 %copy-start.25 = (bf16[768,16]{0,1:T(8,128)(2,1)S(1)}, bf16[768,16]{0,1:T(8,128)(2,1)}, u32[]{:S(2)}) copy-start(bf16[768,16]{0,1:T(8,128)(2,1)} %copy-done.24) | copy-start | bytes 73732
  539.9 18.5 %all-to-all-start.1 = ((bf16[96,8,512]{2,0,1:T(8,128)(2,1)}), bf16[96,8,512]{2,0,1:T(8,128)(2,1)S(1)}, u32[]{:S(2)}, u32[]{:S(2)}) async-start(bf16[96,8,512]{2,0,1:T(8,128)(2,1)} %pad_maximum_fusion.1), calls=%async_computation.1 | async-start | bytes 1572864 | tf_op jit(solution)/shard_map/all_to_all | solution.py:178
  558.4 3.1 copy-start.1
  (4 other events, 5.7 us)
Sparse Core Ops, SparseCore 0:
  58.9 89.7 all-gather.2
  150.9 89.5 all-gather.4
  286.9 82.4 all-reduce.6
  372.7 81.1 reduce-scatter.6
  457.2 80.4 reduce-scatter.8
where the time goes:
time: 576 us; the launch traced here: 568 us
  waiting for transfers between devices  324 us (56%)
  matrix products  136 us (24%)
  blocking collectives  45.7 us (8%)
  local copies, waits for them, and re-layouts  33 us (6%)
  between operations  15.6 us (3%)
  other arithmetic  6.67 us (1%)
  starting transfers between devices  6.65 us (1%)
    unnamed x8, waiting for transfers between devices  182 us
    dot_general x40, matrix products, contract_pair(): lax.dot_general(left, right, (((left_axis,), (right_axis,)), ((), ())), p...  136 us
    all_gather x2, waiting for transfers between devices, local(): gathered = lax.all_gather(part, 'dp', axis=0, tiled=True)  131 us
    all_to_all x1, blocking collectives, local(): lax.all_to_all(send_both, 'expert', split_axis=0, concat_axis=2, tiled=True)  27.4 us
    all_gather x1, blocking collectives, local(): lax.all_gather(lora_part, 'dp', axis=0, tiled=True).astype(jnp.float32)  18.3 us
  transfers between devices with their start and end apart: 6, of which 6 were waited for; matrix products, arithmetic and copies ran while one was open for 17% of the time, Pallas kernels for 0%

commit v1 on v0

--- a/solution.py
+++ b/solution.py
@@ -149,7 +149,11 @@
     owned_total = None
     for c in range(chunks):
         part = recv_both[c * piece : (c + 1) * piece]
-        gathered = lax.all_gather(part, "dp", axis=0, tiled=True)
+        size = lax.axis_size("dp")
+        repeats = [size if d == 0 else 1 for d in range(part.ndim)]
+        gathered = lax.all_to_all(
+            jnp.tile(part, repeats), "dp", split_axis=0, concat_axis=0, tiled=True
+        )
         x_rows = gathered[:, :complete_width]
         dy_rows = gathered[:, complete_width:]
         rows_out, shared_slice, owned_slice = rows_backward_pass(x_rows, dy_rows, params)

time: 576 us -> 919 us (1.60)
  waiting for transfers between devices: 324 us -> 622 us
  starting transfers between devices: 6.65 us -> 25.7 us
  matrix products: 136 us -> 153 us
    all_to_all x0 -> x2, waiting for transfers between devices: none -> 415 us  [local(): lax.all_to_all(jnp.tile(part, repeats), 'dp', split_axis=0, concat_axis=0...]
    all_gather x2 -> x0, waiting for transfers between devices: 131 us -> none  [local(): gathered = lax.all_gather(part, 'dp', axis=0, tiled=True)]
    all_to_all x0 -> x2, starting transfers between devices: none -> 19.1 us  [local(): lax.all_to_all(jnp.tile(part, repeats), 'dp', split_axis=0, concat_axis=0...]
    dot_general x40, matrix products: 136 us -> 153 us  [contract_pair(): lax.dot_general(left, right, (((left_axis,), (right_axis,)), ((), ())), p...]
    unnamed x8 -> x6, waiting for transfers between devices: 182 us -> 195 us
    another operation x0 -> x2, local copies, waits for them, and re-layouts: none -> 12.2 us  [local(): jnp.tile(part, repeats)]
  transfers between devices with their start and end apart: 6 -> 6, of which waited for: 6 -> 6; matrix products, arithmetic and copies ran while one was open for 17% -> 7% of each run, Pallas kernels for 0% -> 0%
where the time goes in v1:
time: 919 us; the launch traced here: 910 us
  waiting for transfers between devices  622 us (68%)
  matrix products  153 us (17%)
  blocking collectives  45.5 us (5%)
  local copies, waits for them, and re-layouts  41.5 us (5%)
  starting transfers between devices  25.7 us (3%)
  between operations  15.2 us (2%)
    all_to_all x2, waiting for transfers between devices, local(): lax.all_to_all(jnp.tile(part, repeats), 'dp', split_axis=0, concat_axis=0...  415 us
    unnamed x6, waiting for transfers between devices  195 us
    dot_general x40, matrix products, contract_pair(): lax.dot_general(left, right, (((left_axis,), (right_axis,)), ((), ())), p...  153 us
    all_to_all x1, blocking collectives, local(): lax.all_to_all(send_both, 'expert', split_axis=0, concat_axis=2, tiled=True)  27.4 us
    all_to_all x2, starting transfers between devices, local(): lax.all_to_all(jnp.tile(part, repeats), 'dp', split_axis=0, concat_axis=0...  19.1 us
  transfers between devices with their start and end apart: 6, of which 6 were waited for; matrix products, arithmetic and copies ran while one was open for 7% of the time, Pallas kernels for 0%

profile of v1, /device:TPU:1, one launch (start us, length us, event | category | flops | bytes accessed | tf_op | source)
XLA Modules:
  0.0 910.0 jit_solution(1147022618846920397)
XLA Ops:
  11.7 1.4 scatter_custom_fusion.1
  13.1 1.4 scatter_custom_fusion
  14.6 5.0 gather_fusion.1
  19.7 2.7 gather_fusion.2
  22.4 2.7 gather_fusion
  25.5 27.4 %all_to_all.38 = bf16[8,96,1024]{2,1,0:T(8,128)(2,1)S(1)} all-to-all(bf16[8,96,1024]{2,1,0:T(8,128)(2,1)S(1)} %pad_maximum_fusion), channel_id=1, replica_groups=mesh['dp'=16,'expert'=8] {'expert'}, dimensions={0} | all-to-all | bytes 3145728 | tf_op jit(solution)/shard_map/all_to_all | solution.py:144
  54.1 1.7 copy.71
  55.8 1.3 fusion.132
  57.7 6.1 tile.30
  63.8 6.8 all-to-all-start.1
  71.2 218.9 %all-to-all-done.1 = bf16[16,48,8192]{2,1,0:T(8,128)(2,1)} async-done(((bf16[16,48,8192]{2,1,0:T(8,128)(2,1)}), bf16[16,48,8192]{2,1,0:T(8,128)(2,1)}, u32[]{:S(2)}, u32[]{:S(2)}) %all-to-all-start.1) | async-done | bytes 12582944 | tf_op jit(solution)/shard_map/all_to_all | solution.py:154
  290.1 6.2 tile.32
  296.3 12.3 %all-to-all-start.2 = ((bf16[16,48,8192]{2,1,0:T(8,128)(2,1)}), bf16[16,48,8192]{2,1,0:T(8,128)(2,1)}, u32[]{:S(2)}, u32[]{:S(2)}) async-start(bf16[16,48,8192]{2,1,0:T(8,128)(2,1)} %tile.32), calls=%async_computation.2 | async-start | bytes 25165824 | tf_op jit(solution)/shard_map/all_to_all | solution.py:154
  308.8 4.7 fusion.88
  313.5 5.8 fusion.10
  319.3 196.6 %all-to-all-done.2 = bf16[16,48,8192]{2,1,0:T(8,128)(2,1)} async-done(((bf16[16,48,8192]{2,1,0:T(8,128)(2,1)}), bf16[16,48,8192]{2,1,0:T(8,128)(2,1)}, u32[]{:S(2)}, u32[]{:S(2)}) %all-to-all-start.2) | async-done | bytes 12582944 | tf_op jit(solution)/shard_map/all_to_all | solution.py:154
  515.9 4.7 fusion.91
  520.6 5.9 fusion.4
  526.5 4.5 fusion.79
  531.0 4.7 fusion.85
  535.7 6.1 fusion.31
  541.8 5.9 fusion.27
  547.6 4.5 fusion.76
  552.1 4.7 fusion.82
  556.8 5.8 fusion.39
  562.7 5.8 fusion.35
  569.8 1.8 multiply_convert_fusion.1
  571.8 6.4 fusion.29
  578.4 6.4 fusion.37
  584.8 3.7 fusion.53
  589.3 1.8 multiply_convert_fusion
  591.9 4.4 fusion.51
  597.2 4.1 fusion
  601.2 4.4 fusion.23
  605.7 4.4 fusion.24
  610.1 4.1 fusion.20
  616.7 12.0 %add_convert_fusion.1 = bf16[768,4096]{1,0:T(8,128)(2,1)} fusion(f32[768,4096]{1,0:T(8,128)} %fusion.29, f32[768,4096]{1,0:T(8,128)} %fusion.37, bf16[16,4096]{1,0:T(8,128)(2,1)S(1)} %bitcast.182, bf16[16,4096]{1,0:T(8,128)(2,1)S(1)} %bitcast.180, bf16[16,768]{1,0:T(8,128)(2,1)} %bitcast.188, bf16[16,768]{1,0:T(8,128)(2,1)} %bitcast.187), kind=kOutput, calls=%fused_computation.7 | convolution fusion | flops 214532096 | bytes 31768576 | tf_op jit(solution)/shard_map/dot_general | solution.py:11
  628.7 8.6 fusion.25
  637.4 6.4 fusion.33
  643.8 12.0 %add_convert_fusion = bf16[768,4096]{1,0:T(8,128)(2,1)} fusion(f32[768,4096]{1,0:T(8,128)} %fusion.25, f32[768,4096]{1,0:T(8,128)} %fusion.33, bf16[16,4096]{1,0:T(8,128)(2,1)S(1)} %bitcast.183, bf16[16,4096]{1,0:T(8,128)(2,1)S(1)} %bitcast.181, bf16[16,768]{1,0:T(8,128)(2,1)S(1)} %bitcast.189, bf16[16,768]{1,0:T(8,128)(2,1)S(1)} %bitcast.186), kind=kOutput, calls=%fused_computation.6 | convolution fusion | flops 214532096 | bytes 31768576 | tf_op jit(solution)/shard_map/dot_general | solution.py:11
  657.9 1.4 fusion.135
  659.3 2.1 fusion.95
  663.9 46.9 %all-reduce.7.cloned.1.call-done = bf16[128,1536]{1,0:T(8,128)(2,1)} async-done(((bf16[128,1536]{1,0:T(8,128)(2,1)}), bf16[128,1536]{1,0:T(8,128)(2,1)}) %all-reduce.7.cloned.1.call-update) | async-done | bytes 393232
  711.5 18.1 %all_gather.3 = bf16[128,1536]{1,0:T(8,128)(2,1)S(1)} all-gather(bf16[8,1536]{1,0:T(8,128)(2,1)S(1)} %constant_dynamic-slice_fusion), channel_id=1, replica_groups=mesh['dp'=16,'expert'=8] {'dp'}, dimensions={0}, use_global_device_ids=true | all-gather | bytes 417792 | tf_op jit(solution)/shard_map/all_gather | solution.py:177
  730.0 65.5 %reduce-scatter.7.cloned.1.call-done = bf16[1,48,4096]{2,1,0:T(8,128)(2,1)} async-done(((bf16[16,48,4096]{2,1,0:T(8,128)(2,1)}), bf16[1,48,4096]{2,1,0:T(8,128)(2,1)}) %reduce-scatter.7.cloned.1.call-update) | async-done | bytes 393232
  796.8 82.8 %reduce-scatter.9.cloned.1.call-done = bf16[1,48,4096]{2,1,0:T(8,128)(2,1)} async-done(((bf16[16,48,4096]{2,1,0:T(8,128)(2,1)}), bf16[1,48,4096]{2,1,0:T(8,128)(2,1)}) %reduce-scatter.9.cloned.1.call-update) | async-done | bytes 393232
  881.8 6.2 all-to-all-start.3
  888.8 11.4 %all-to-all-done.3 = bf16[96,8,512]{2,0,1:T(8,128)(2,1)S(1)} async-done(((bf16[96,8,512]{2,0,1:T(8,128)(2,1)}), bf16[96,8,512]{2,0,1:T(8,128)(2,1)S(1)}, u32[]{:S(2)}, u32[]{:S(2)}) %all-to-all-start.3) | async-done | bytes 786464 | tf_op jit(solution)/shard_map/all_to_all | solution.py:182
  (133 shorter events, 26.6 us)
Async XLA Ops:
  7.2 301.6 %copy-start = (bf16[1,4096,16]{1,2,0:T(8,128)(2,1)S(1)}, bf16[1,4096,16]{1,2,0:T(8,128)(2,1)}, u32[]{:S(2)}) copy-start(bf16[1,4096,16]{1,2,0:T(8,128)(2,1)} %param.25) | copy-start | bytes 393220
  7.2 12.4 %copy-start.15 = (bf16[128,512]{1,0:T(8,128)(2,1)S(1)}, bf16[128,512]{1,0:T(8,128)(2,1)}, u32[]{:S(2)}) copy-start(bf16[128,512]{1,0:T(8,128)(2,1)} %param.14) | copy-start | bytes 393220
  7.2 12.5 %copy-start.16 = (bf16[128,512]{1,0:T(8,128)(2,1)S(1)}, bf16[128,512]{1,0:T(8,128)(2,1)}, u32[]{:S(2)}) copy-start(bf16[128,512]{1,0:T(8,128)(2,1)} %param.13) | copy-start | bytes 393220
  63.8 226.3 %all-to-all-start.1 = ((bf16[16,48,8192]{2,1,0:T(8,128)(2,1)}), bf16[16,48,8192]{2,1,0:T(8,128)(2,1)}, u32[]{:S(2)}, u32[]{:S(2)}) async-start(bf16[16,48,8192]{2,1,0:T(8,128)(2,1)} %tile.30), calls=%async_computation.1 | async-start | bytes 25165824 | tf_op jit(solution)/shard_map/all_to_all | solution.py:154
  296.3 219.6 %all-to-all-start.2 = ((bf16[16,48,8192]{2,1,0:T(8,128)(2,1)}), bf16[16,48,8192]{2,1,0:T(8,128)(2,1)}, u32[]{:S(2)}, u32[]{:S(2)}) async-start(bf16[16,48,8192]{2,1,0:T(8,128)(2,1)} %tile.32), calls=%async_computation.2 | async-start | bytes 25165824 | tf_op jit(solution)/shard_map/all_to_all | solution.py:154
  308.6 402.2 %all-reduce.7.cloned.1.call-start = ((), (), s32[]{:S(2)}) async-start(), calls=%async_computation.6 | async-start | bytes 786432
  308.8 4.7 copy-start.31
  313.5 255.5 %copy-start.21 = (bf16[768,16]{0,1:T(8,128)(2,1)}, bf16[768,16]{0,1:T(8,128)(2,1)S(1)}, u32[]{:S(2)}) copy-start(bf16[768,16]{0,1:T(8,128)(2,1)S(1)} %fusion.88) | copy-start | bytes 73732
  515.9 4.7 copy-start.32
  520.6 67.9 %copy-start.23 = (bf16[768,16]{0,1:T(8,128)(2,1)}, bf16[768,16]{0,1:T(8,128)(2,1)S(1)}, u32[]{:S(2)}) copy-start(bf16[768,16]{0,1:T(8,128)(2,1)S(1)} %fusion.91) | copy-start | bytes 73732
  520.6 5.9 copy-start.6
  531.0 37.6 %copy-start.19 = (bf16[768,16]{0,1:T(8,128)(2,1)}, bf16[768,16]{0,1:T(8,128)(2,1)S(1)}, u32[]{:S(2)}) copy-start(bf16[768,16]{0,1:T(8,128)(2,1)S(1)} %fusion.79) | copy-start | bytes 73732
  531.0 4.7 copy-start.2
  535.7 53.2 %copy-start.17 = (bf16[768,16]{0,1:T(8,128)(2,1)}, bf16[768,16]{0,1:T(8,128)(2,1)S(1)}, u32[]{:S(2)}) copy-start(bf16[768,16]{0,1:T(8,128)(2,1)S(1)} %fusion.85) | copy-start | bytes 73732
  541.7 5.9 copy-start.7
  552.1 17.7 %copy-start.28 = (bf16[768,16]{0,1:T(8,128)(2,1)}, bf16[768,16]{0,1:T(8,128)(2,1)S(1)}, u32[]{:S(2)}) copy-start(bf16[768,16]{0,1:T(8,128)(2,1)S(1)} %fusion.76) | copy-start | bytes 73732
  552.1 4.7 copy-start.3
  556.8 32.5 %copy-start.26 = (bf16[768,16]{0,1:T(8,128)(2,1)}, bf16[768,16]{0,1:T(8,128)(2,1)S(1)}, u32[]{:S(2)}) copy-start(bf16[768,16]{0,1:T(8,128)(2,1)S(1)} %fusion.82) | copy-start | bytes 73732
  562.7 5.9 copy-start.9
  562.7 6.3 copy-start.8
  568.6 1.2 copy-start.25
  571.8 13.0 %copy-start.11 = (bf16[768,16]{0,1:T(8,128)(2,1)}, bf16[768,16]{0,1:T(8,128)(2,1)S(1)}, u32[]{:S(2)}) copy-start(bf16[768,16]{0,1:T(8,128)(2,1)S(1)} %convolution_convert_fusion.5) | copy-start | bytes 73732
  578.4 13.5 %copy-start.12 = (bf16[768,16]{0,1:T(8,128)(2,1)}, bf16[768,16]{0,1:T(8,128)(2,1)S(1)}, u32[]{:S(2)}) copy-start(bf16[768,16]{0,1:T(8,128)(2,1)S(1)} %convolution_convert_fusion.4) | copy-start | bytes 73732
  601.2 4.4 copy-start.5
  601.2 4.4 copy-start.13
  616.4 179.1 %reduce-scatter.7.cloned.1.call-start = ((), (), s32[]{:S(2)}) async-start(), calls=%async_computation.7 | async-start | bytes 6684672
  628.7 250.9 %reduce-scatter.9.cloned.1.call-start = ((), (), s32[]{:S(2)}) async-start(), calls=%async_computation.8 | async-start | bytes 6684672
  628.7 8.7 copy-start.4
  637.4 6.4 copy-start.10
  637.4 6.4 copy-start.14
  655.8 0.6 copy-start.30
  655.8 0.9 copy-start.33
  655.8 2.1 copy-start.22
  655.8 3.5 copy-start.24
  655.8 5.6 copy-start.29
  655.8 5.9 copy-start.27
  655.8 6.8 copy-start.20
  655.8 7.1 copy-start.18
  881.8 18.5 %all-to-all-start.3 = ((bf16[96,8,512]{2,0,1:T(8,128)(2,1)}), bf16[96,8,512]{2,0,1:T(8,128)(2,1)S(1)}, u32[]{:S(2)}, u32[]{:S(2)}) async-start(bf16[96,8,512]{2,0,1:T(8,128)(2,1)} %pad_maximum_fusion.1), calls=%async_computation.3 | async-start | bytes 1572864 | tf_op jit(solution)/shard_map/all_to_all | solution.py:182
  900.2 3.1 copy-start.1
Sparse Core Ops, SparseCore 0:
  616.5 94.1 all-reduce.6
  714.2 81.3 reduce-scatter.6
  799.0 80.5 reduce-scatter.8
